TPU v7x, 128 devices: a whole 4x4x4 slice. The times are simulated.
128 devices in a mesh: dp: 8 (over x, core), fsdp: 16 (over z, y).
Axes of the slice: x: 4, y: 4, z: 4, core: 2. Of those that a mesh axis runs over, the one named last changes fastest.
Arguments:
- hidden_rows: bfloat16 [2048, 15360], P('fsdp', 'dp'), may hold values from -6 to 6
- upstream: bfloat16 [2048, 4096], P('fsdp'), may hold values from -6 to 6
- advantages: float32 [16, 4], P('fsdp'), may hold values from -4 to 4
- lengths: int32 [16, 4], P('fsdp'), may hold values from 1 to 64, 128 in all within a row
- dest_rank: int32 [256, 1], P('fsdp'), may hold values from 0 to 15; in each aligned block of 16 rows (0 to 15, 16 to 31, ...) at most 2 rows name the same one
- w_down: bfloat16 [15360, 4096], P('dp', 'fsdp'), may hold values from -0.046875 to 0.046875
Outputs:
- packed_out: bfloat16 [4096, 4096], P('fsdp', 'dp')
- packed_back: bfloat16 [4096, 15360], P('fsdp', 'dp')
- weight_grad: float32 [15360, 4096], P('dp', 'fsdp')
Inputs may be any that keep to these rules, and one draw needn't show every extreme that they name: Each generator group's 4 lengths sum to 128, the largest is 64. `dest_rank`: among the 16 blocks of one generator group, at most 2 name the same learner rank, and some learner is named 2 times.
All inputs are finite; a program needn't handle non-finite values.
Results may differ from a plain program's by a relative error of at most 0.014.
Values may be sent and summed in bfloat16 or wider, within the bound.
No kernel may reach another device: no remote copies, remote signals or barrier semaphores. Data moves between devices by JAX's collectives and lax.ppermute only.
A program may use at most 128 MiB of HBM per device.

v0:
```python
import jax
import jax.numpy as jnp
from jax import lax
from jax.sharding import PartitionSpec as P

SENDB = 2


def rounded(value):
    return lax.optimization_barrier(value.astype(jnp.bfloat16)).astype(jnp.float32)


def on_device(hidden_rows, upstream, advantages, lengths, dest_rank, w_down):
    groups = lax.axis_size("fsdp")
    src_rows = hidden_rows.shape[0]
    per_group = lengths.shape[1]
    blocks = dest_rank.shape[0]
    block_rows = src_rows // blocks
    ends_at = jnp.cumsum(lengths[0])
    starts = ends_at - lengths[0]
    position = jnp.arange(src_rows, dtype=jnp.int32)[:, None]
    member = (position >= starts[None, :]) & (position < ends_at[None, :])
    factor = advantages[0] * (src_rows / (per_group * lengths[0].astype(jnp.float32)))
    row_weight = jnp.sum(jnp.where(member, factor[None, :], jnp.float32(0.0)), axis=1)
    scaled = (row_weight[:, None] * upstream.astype(jnp.float32)).astype(jnp.bfloat16)
    w_full = lax.all_gather(w_down, "fsdp", axis=1, tiled=True)
    partial_value = lax.dot_general(
        hidden_rows, scaled, (((0,), (0,)), ((), ())), preferred_element_type=jnp.float32
    )
    weight_grad = lax.psum_scatter(
        rounded(partial_value).astype(jnp.bfloat16), "fsdp", scatter_dimension=1, tiled=True
    ).astype(jnp.float32) / (per_group * groups)
    target = dest_rank[:, 0]
    order = jnp.arange(blocks, dtype=jnp.int32)
    earlier = order[None, :] < order[:, None]
    same = target[:, None] == target[None, :]
    slot_index = jnp.sum((same & earlier).astype(jnp.int32), axis=1)
    target_slot = target * SENDB + slot_index
    one_hot = (target_slot[None, :] == jnp.arange(groups * SENDB, dtype=jnp.int32)[:, None]).astype(
        jnp.bfloat16
    )

    def place_blocks(values):
        pieces = values.reshape(blocks, block_rows, values.shape[1])
        placed = jnp.einsum(
            "ps,sbc->pbc", one_hot, pieces, preferred_element_type=jnp.float32
        ).astype(values.dtype)
        return placed.reshape(groups, SENDB * block_rows, values.shape[1])

    hidden_recv, scaled_recv = (
        lax.all_to_all(place_blocks(hidden_rows), "fsdp", split_axis=0, concat_axis=0, tiled=True),
        lax.all_to_all(place_blocks(scaled), "fsdp", split_axis=0, concat_axis=0, tiled=True),
    )
    hidden_flat = hidden_recv.reshape(-1, hidden_recv.shape[2])
    scaled_flat = scaled_recv.reshape(-1, scaled_recv.shape[2])
    forward_part = rounded(jnp.dot(hidden_flat, w_full, preferred_element_type=jnp.float32))
    packed_out = lax.psum_scatter(
        forward_part.astype(jnp.bfloat16), "dp", scatter_dimension=1, tiled=True
    )
    packed_back = lax.dot_general(
        scaled_flat, w_full, (((1,), (1,)), ((), ())), preferred_element_type=jnp.float32
    ).astype(jnp.bfloat16)
    return (packed_out, packed_back, weight_grad)


def solution(mesh):
    placed = (
        P("fsdp", "dp"),
        P("fsdp", None),
        P("fsdp", None),
        P("fsdp", None),
        P("fsdp", None),
        P("dp", "fsdp"),
    )
    return jax.shard_map(
        on_device,
        mesh=mesh,
        in_specs=placed,
        out_specs=(P("fsdp", "dp"), P("fsdp", "dp"), P("dp", "fsdp")),
        check_vma=False,
    )
```

profile of v0, /device:TPU:0, one launch (start us, length us, event | category | flops | bytes accessed | tf_op | source)
XLA Modules:
  0.0 309.7 jit_solution(16889025768865290448)
XLA Ops:
  7.2 0.0 copy-start
  7.2 0.0 all-gather.2.cloned.1.call-start
  7.2 0.7 all-gather.2.cloned.1.call-update
  7.9 0.0 reduce-scatter.5.cloned.1.call-start
  8.0 0.8 reduce-window.4
  8.8 0.7 fusion.11
  9.5 0.7 fusion.10
  10.1 0.1 select_reduce_fusion
  10.2 0.0 copy-done
  10.2 9.4 %convert_bitcast_fusion = bf16[1920,4096]{0,1:T(8,128)(2,1)} fusion(bf16[128,1920]{1,0:T(8,128)(2,1)S(1)} %copy-done, bf16[128,4096]{1,0:T(8,128)(2,1)} %param.7, f32[128]{0:T(128)S(1)} %select_reduce_fusion), kind=kOutput, calls=%fused_computation | convolution fusion | flops 2022703104 | bytes 17269248 | tf_op jit(solution)/shard_map/dot_general | solution.py:27
  19.6 0.0 copy-start.2
  19.6 0.0 reduce-scatter.5.cloned.1.call-update
  19.7 0.0 reduce-scatter.3.cloned.1.call-start
  19.7 0.6 copy-done.2
  20.3 0.2 convert_reduce_fusion
  20.5 0.5 convolution_convert_fusion.3
  21.0 0.3 copy.18
  21.3 29.7 %all_to_all.10 = bf16[16,16,1920]{2,1,0:T(8,128)(2,1)S(1)} all-to-all(bf16[16,16,1920]{2,1,0:T(8,128)(2,1)S(1)} %bitcast.32), channel_id=1, replica_groups=mesh['dp'=8,'fsdp'=16] {'fsdp'}, dimensions={0} | all-to-all | bytes 1966080 | tf_op jit(solution)/shard_map/all_to_all | solution.py:51
  51.0 85.3 %all-gather.2.cloned.1.call-done = bf16[1920,4096]{1,0:T(8,128)(2,1)} async-done(((bf16[1920,256]{1,0:T(8,128)(2,1)}), bf16[1920,4096]{1,0:T(8,128)(2,1)}) %all-gather.2.cloned.1.call-update) | async-done | bytes 15728656 | tf_op jit(solution)/shard_map/all_gather | solution.py:26
  136.4 11.5 %convolution_convert_fusion = bf16[256,4096]{1,0:T(8,128)(2,1)} fusion(bf16[256,1920]{1,0:T(8,128)(2,1)S(1)} %bitcast.34, bf16[1920,4096]{1,0:T(8,128)(2,1)} %all-gather.2.cloned.1.call-done), kind=kOutput, calls=%fused_computation.1 | convolution fusion | flops 4027580416 | bytes 18808832 | tf_op jit(solution)/shard_map/dot_general | solution.py:56
  147.8 0.0 copy-start.1
  147.8 0.0 reduce-scatter.3.cloned.1.call-update
  147.9 1.5 copy-done.1
  149.4 0.3 fusion.2
  149.6 1.4 convolution_convert_fusion.1
  151.1 1.2 copy.20
  152.2 50.2 %all_to_all.11 = bf16[16,16,4096]{2,1,0:T(8,128)(2,1)S(1)} all-to-all(bf16[16,16,4096]{2,1,0:T(8,128)(2,1)S(1)} %bitcast.31), channel_id=1, replica_groups=mesh['dp'=8,'fsdp'=16] {'fsdp'}, dimensions={0} | all-to-all | bytes 4194304 | tf_op jit(solution)/shard_map/all_to_all | solution.py:52
  202.4 9.7 %convolution_convert_fusion.2 = bf16[256,1920]{1,0:T(8,128)(2,1)} fusion(bf16[256,4096]{1,0:T(8,128)(2,1)S(1)} %bitcast.33, bf16[1920,4096]{1,0:T(8,128)(2,1)} %all-gather.2.cloned.1.call-done), kind=kOutput, calls=%fused_computation.3 | convolution fusion | flops 4027023360 | bytes 18808832 | tf_op jit(solution)/shard_map/dot_general | solution.py:60
  212.0 55.4 %reduce-scatter.5.cloned.1.call-done = bf16[1920,256]{0,1:T(8,128)(2,1)} async-done(((bf16[1920,4096]{0,1:T(8,128)(2,1)}), bf16[1920,256]{0,1:T(8,128)(2,1)}) %reduce-scatter.5.cloned.1.call-update) | async-done | bytes 983056 | tf_op jit(solution)/shard_map/reduce_scatter | solution.py:30
  267.5 1.3 convert_multiply_fusion
  268.8 1.8 copy.21
  270.6 32.5 %reduce-scatter.3.cloned.1.call-done = bf16[256,512]{1,0:T(8,128)(2,1)} async-done(((bf16[256,4096]{1,0:T(8,128)(2,1)}), bf16[256,512]{1,0:T(8,128)(2,1)}) %reduce-scatter.3.cloned.1.call-update) | async-done | bytes 262160 | tf_op jit(solution)/shard_map/reduce_scatter | solution.py:57
  (1 shorter events, 0.0 us)
Async XLA Ops:
  7.2 3.1 copy-start
  7.2 129.2 %all-gather.2.cloned.1.call-start = ((), (), s32[]{:S(2)}) async-start(), calls=%async_computation.4 | async-start | bytes 16711680 | tf_op jit(solution)/shard_map/all_gather | solution.py:26
  7.9 259.6 %reduce-scatter.5.cloned.1.call-start = ((), (), s32[]{:S(2)}) async-start(), calls=%async_computation.6 | async-start | bytes 16711680 | tf_op jit(solution)/shard_map/reduce_scatter | solution.py:30
  19.6 0.7 copy-start.2
  19.7 283.5 %reduce-scatter.3.cloned.1.call-start = ((), (), s32[]{:S(2)}) async-start(), calls=%async_computation.5 | async-start | bytes 2359296 | tf_op jit(solution)/shard_map/reduce_scatter | solution.py:57
  147.8 1.5 copy-start.1
Sparse Core Ops, SparseCore 0:
  10.1 126.2 all-gather.1
  139.8 127.6 reduce-scatter.4
  270.5 32.6 reduce-scatter.2
where the time goes:
time: 310 us
  waiting for transfers between devices  174 us (56%)
  blocking collectives  79.9 us (26%)
  matrix products  32.5 us (10%)
  between operations  13.8 us (4%)
  local copies, waits for them, and re-layouts  5.33 us (2%)
  other arithmetic  4.03 us (1%)
    all_gather x1, waiting for transfers between devices, on_device(): w_full = lax.all_gather(w_down, 'fsdp', axis=1, tiled=True)  85.3 us
    reduce_scatter x1, waiting for transfers between devices, on_device(): lax.psum_scatter(rounded(partial_value).astype(jnp.bfloat16), 'fsdp', sca...  55.4 us
    all_to_all x1, blocking collectives, on_device(): lax.all_to_all(place_blocks(scaled), 'fsdp', split_axis=0, concat_axis=0,...  50.2 us
    reduce_scatter x1, waiting for transfers between devices, on_device(): lax.psum_scatter(forward_part.astype(jnp.bfloat16), 'dp', scatter_dimensi...  32.5 us
    all_to_all x1, blocking collectives, on_device(): lax.all_to_all(place_blocks(hidden_rows), 'fsdp', split_axis=0, concat_ax...  29.7 us
    dot_general x1, matrix products, on_device(): jnp.dot(hidden_flat, w_full, preferred_element_type=jnp.float32)  11.5 us
    dot_general x1, matrix products, on_device(): lax.dot_general(scaled_flat, w_full, (((1,), (1,)), ((), ())), preferred_...  9.67 us
    dot_general x1, matrix products, on_device(): lax.dot_general(hidden_rows, scaled, (((0,), (0,)), ((), ())), preferred_...  9.42 us
  transfers between devices with their start and end apart: 3, of which 3 were waited for; matrix products, arithmetic and copies ran while one was open for 13% of the time, Pallas kernels for 0%

commit v1 on v0

--- a/solution.py
+++ b/solution.py
@@ -23,7 +23,10 @@
     factor = advantages[0] * (src_rows / (per_group * lengths[0].astype(jnp.float32)))
     row_weight = jnp.sum(jnp.where(member, factor[None, :], jnp.float32(0.0)), axis=1)
     scaled = (row_weight[:, None] * upstream.astype(jnp.float32)).astype(jnp.bfloat16)
-    w_full = lax.all_gather(w_down, "fsdp", axis=1, tiled=True)
+    peers = lax.axis_size("fsdp")
+    parts = jnp.stack([w_down for _ in range(peers)])
+    parts = lax.all_to_all(parts, "fsdp", split_axis=0, concat_axis=0)
+    w_full = jnp.concatenate(parts, axis=1)
     partial_value = lax.dot_general(
         hidden_rows, scaled, (((0,), (0,)), ((), ())), preferred_element_type=jnp.float32
     )

time: 310 us -> 349 us (1.13)
  blocking collectives: 79.9 us -> 250 us
  waiting for transfers between devices: 174 us -> 25.5 us
  starting transfers between devices: 0.12 us -> 8.21 us
  matrix products: 32.5 us -> 37.3 us
    all_to_all x1, blocking collectives: 29.7 us -> 220 us  [on_device(): parts = lax.all_to_all(parts, 'fsdp', split_axis=0, concat_axis=0)]
    all_gather x1 -> x0, waiting for transfers between devices: 85.3 us -> none  [on_device(): w_full = lax.all_gather(w_down, 'fsdp', axis=1, tiled=True)]
    reduce_scatter x1, waiting for transfers between devices: 55.4 us -> 0.01 us  [on_device(): lax.psum_scatter(rounded(partial_value).astype(jnp.bfloat16), 'fsdp', sca...]
    reduce_scatter x1, waiting for transfers between devices: 32.5 us -> 0.01 us  [on_device(): lax.psum_scatter(forward_part.astype(jnp.bfloat16), 'dp', scatter_dimensi...]
    all_to_all x0 -> x1, waiting for transfers between devices: none -> 25.5 us  [on_device(): lax.all_to_all(place_blocks(hidden_rows), 'fsdp', split_axis=0, concat_ax...]
    all_to_all x1, blocking collectives: 50.2 us -> 30.4 us  [on_device(): lax.all_to_all(place_blocks(scaled), 'fsdp', split_axis=0, concat_axis=0,...]
    all_to_all x0 -> x1, starting transfers between devices: none -> 8.13 us  [on_device(): lax.all_to_all(place_blocks(hidden_rows), 'fsdp', split_axis=0, concat_ax...]
    dot_general x1, matrix products: 11.5 us -> 16.8 us  [on_device(): jnp.dot(hidden_flat, w_full, preferred_element_type=jnp.float32)]
  transfers between devices with their start and end apart: 3 -> 3, of which waited for: 3 -> 1; matrix products, arithmetic and copies ran while one was open for 13% -> 10% of each run, Pallas kernels for 0% -> 0%
where the time goes in v1:
time: 349 us; the launch traced here: 348 us
  blocking collectives  250 us (72%)
  matrix products  37.3 us (11%)
  waiting for transfers between devices  25.5 us (7%)
  between operations  14.1 us (4%)
  local copies, waits for them, and re-layouts  8.77 us (3%)
  starting transfers between devices  8.21 us (2%)
  other arithmetic  4.13 us (1%)
    all_to_all x1, blocking collectives, on_device(): parts = lax.all_to_all(parts, 'fsdp', split_axis=0, concat_axis=0)  220 us
    all_to_all x1, blocking collectives, on_device(): lax.all_to_all(place_blocks(scaled), 'fsdp', split_axis=0, concat_axis=0,...  30.4 us
    all_to_all x1, waiting for transfers between devices, on_device(): lax.all_to_all(place_blocks(hidden_rows), 'fsdp', split_axis=0, concat_ax...  25.5 us
    dot_general x1, matrix products, on_device(): jnp.dot(hidden_flat, w_full, preferred_element_type=jnp.float32)  16.8 us
    dot_general x1, matrix products, on_device(): lax.dot_general(hidden_rows, scaled, (((0,), (0,)), ((), ())), preferred_...  9.53 us
    dot_general x1, matrix products, on_device(): lax.dot_general(scaled_flat, w_full, (((1,), (1,)), ((), ())), preferred_...  9.06 us
    all_to_all x1, starting transfers between devices, on_device(): lax.all_to_all(place_blocks(hidden_rows), 'fsdp', split_axis=0, concat_ax...  8.13 us
  transfers between devices with their start and end apart: 3, of which 1 were waited for; matrix products, arithmetic and copies ran while one was open for 10% of the time, Pallas kernels for 0%

profile of v1, /device:TPU:0, one launch (start us, length us, event | category | flops | bytes accessed | tf_op | source)
XLA Modules:
  0.0 348.5 jit_solution(14597172058874316812)
XLA Ops:
  7.2 0.0 copy-start
  7.2 0.0 reduce-scatter.5.cloned.1.call-start
  7.2 0.7 fusion.11
  8.0 0.8 reduce-window.4
  8.8 0.7 fusion.10
  9.4 0.1 select_reduce_fusion
  9.5 0.0 copy-done
  9.5 9.5 %convert_bitcast_fusion = bf16[1920,4096]{0,1:T(8,128)(2,1)} fusion(bf16[128,1920]{1,0:T(8,128)(2,1)S(1)} %copy-done, bf16[128,4096]{1,0:T(8,128)(2,1)} %param.7, f32[128]{0:T(128)S(1)} %select_reduce_fusion), kind=kOutput, calls=%fused_computation | convolution fusion | flops 2022703104 | bytes 17269248 | tf_op jit(solution)/shard_map/dot_general | solution.py:30
  19.1 0.0 reduce-scatter.5.cloned.1.call-update
  19.1 0.6 copy-done.4
  19.7 0.2 convert_reduce_fusion
  19.9 0.5 convolution_convert_fusion.3
  20.4 0.0 copy-start.3
  20.5 1.2 copy.19
  21.7 8.1 %all-to-all-start = ((bf16[16,16,1920]{2,1,0:T(8,128)(2,1)}), bf16[16,16,1920]{2,1,0:T(8,128)(2,1)S(1)}, u32[]{:S(2)}, u32[]{:S(2)}) async-start(bf16[16,16,1920]{2,1,0:T(8,128)(2,1)} %bitcast.3), calls=%async_computation | async-start | bytes 1966080 | tf_op jit(solution)/shard_map/all_to_all | solution.py:54
  29.8 0.0 reduce-scatter.3.cloned.1.call-start
  29.9 0.0 copy-done.3
  29.9 0.7 copy.20
  30.6 25.5 %all-to-all-done = bf16[16,16,1920]{2,1,0:T(8,128)(2,1)S(1)} async-done(((bf16[16,16,1920]{2,1,0:T(8,128)(2,1)}), bf16[16,16,1920]{2,1,0:T(8,128)(2,1)S(1)}, u32[]{:S(2)}, u32[]{:S(2)}) %all-to-all-start) | async-done | bytes 983072 | tf_op jit(solution)/shard_map/all_to_all | solution.py:54
  56.1 2.0 stack.2
  58.1 220.0 %all_to_all.15 = bf16[16,1920,256]{1,2,0:T(8,128)(2,1)} all-to-all(bf16[16,1920,256]{1,2,0:T(8,128)(2,1)S(1)} %stack.2), channel_id=1, replica_groups=mesh['dp'=8,'fsdp'=16] {'fsdp'}, dimensions={0} | all-to-all | bytes 31457280 | tf_op jit(solution)/shard_map/all_to_all | solution.py:28
  278.1 16.8 %convolution_convert_fusion = bf16[256,4096]{1,0:T(8,128)(2,1)} fusion(bf16[256,1920]{1,0:T(8,128)(2,1)S(1)} %bitcast.38, bf16[1920,4096]{0,1:T(8,128)(2,1)} %bitcast.34), kind=kOutput, calls=%fused_computation.1 | convolution fusion | flops 4027580416 | bytes 18808832 | tf_op jit(solution)/shard_map/dot_general | solution.py:59
  294.9 0.0 reduce-scatter.3.cloned.1.call-update
  295.0 1.2 copy-done.2
  296.1 0.3 fusion.2
  296.4 1.4 convolution_convert_fusion.1
  297.8 1.2 copy.22
  299.0 30.4 %all_to_all.16 = bf16[16,16,4096]{2,1,0:T(8,128)(2,1)S(1)} all-to-all(bf16[16,16,4096]{2,1,0:T(8,128)(2,1)S(1)} %bitcast.36), channel_id=1, replica_groups=mesh['dp'=8,'fsdp'=16] {'fsdp'}, dimensions={0} | all-to-all | bytes 4194304 | tf_op jit(solution)/shard_map/all_to_all | solution.py:55
  329.4 9.1 %convolution_convert_fusion.2 = bf16[256,1920]{1,0:T(8,128)(2,1)} fusion(bf16[256,4096]{1,0:T(8,128)(2,1)S(1)} %bitcast.37, bf16[1920,4096]{0,1:T(8,128)(2,1)} %bitcast.35), kind=kOutput, calls=%fused_computation.3 | convolution fusion | flops 4027023360 | bytes 18808832 | tf_op jit(solution)/shard_map/dot_general | solution.py:63
  338.4 1.4 convert_multiply_fusion
  339.8 1.8 copy.23
  341.6 0.0 copy-done.1
  (6 shorter events, 0.0 us)
Async XLA Ops:
  7.2 2.4 copy-start
  7.2 331.3 %reduce-scatter.5.cloned.1.call-start = ((), (), s32[]{:S(2)}) async-start(), calls=%async_computation.6 | async-start | bytes 16711680 | tf_op jit(solution)/shard_map/reduce_scatter | solution.py:33
  19.1 0.7 copy-start.4
  20.4 9.4 %copy-start.3 = (bf16[1920,256]{1,0:T(8,128)(2,1)S(1)}, bf16[1920,256]{1,0:T(8,128)(2,1)}, u32[]{:S(2)}) copy-start(bf16[1920,256]{1,0:T(8,128)(2,1)} %param.11) | copy-start | bytes 2949124
  21.7 34.4 %all-to-all-start = ((bf16[16,16,1920]{2,1,0:T(8,128)(2,1)}), bf16[16,16,1920]{2,1,0:T(8,128)(2,1)S(1)}, u32[]{:S(2)}, u32[]{:S(2)}) async-start(bf16[16,16,1920]{2,1,0:T(8,128)(2,1)} %bitcast.3), calls=%async_computation | async-start | bytes 1966080 | tf_op jit(solution)/shard_map/all_to_all | solution.py:54
  29.8 311.8 %reduce-scatter.3.cloned.1.call-start = ((), (), s32[]{:S(2)}) async-start(), calls=%async_computation.5 | async-start | bytes 2359296 | tf_op jit(solution)/shard_map/reduce_scatter | solution.py:60
  294.9 1.2 copy-start.2
  338.4 3.2 copy-start.1
Sparse Core Ops, SparseCore 0:
  19.2 285.9 reduce-scatter.4
  308.1 33.1 reduce-scatter.2
